TPU v7x, 256 devices: a whole 4x4x8 slice. The times are simulated.
256 devices in a mesh: row: 32 (over x, z), col: 8 (over y, core).
Axes of the slice: x: 4, y: 4, z: 8, core: 2. Of those that a mesh axis runs over, the one named last changes fastest.
Arguments:
- kernel: float32 [2048, 65536], P('row', 'col'), may hold values from -6 to 6
- basis: float32 [65536, 128], P('col', 'row'), may hold values from -0.0234375 to 0.0234375
- responses: float32 [2048, 512], P('row', 'col'), may hold values from -6 to 6
Outputs:
- scores: float32 [2048, 128], P('row')
- loadings: float32 [128, 65536], P('row', 'col')
- weights: float32 [512, 128], P('col')
- deflated: float32 [2048, 65536], P('row', 'col')
- basis_next: float32 [2048, 128], P('row')
All inputs are finite; a program needn't handle non-finite values.
Results may differ from a plain program's by a relative error of at most 0.00012.
Values sent between devices are 32-bit elements; how exact they have to be, the bound alone decides.
No kernel may reach another device: no remote copies, remote signals or barrier semaphores. Data moves between devices by JAX's collectives and lax.ppermute only.
A program may use at most 64 MiB of HBM per device.

v0:
```python
import math
import jax
import jax.numpy as jnp
from jax import lax
from jax.sharding import Mesh
from jax.sharding import PartitionSpec as P

ROW = ("row_0", "row_1")


def sent_to_all(x, axis):
    devices = lax.axis_size(axis)
    return lax.all_to_all(jnp.broadcast_to(x[None], (devices, *x.shape)), axis, 0, 0, tiled=True)


def taken_together(x, axis):
    everything = sent_to_all(x, axis)
    return jnp.sum(everything, axis=0)


def summed_rows(subtotal, axes):
    for axis in axes:
        subtotal = lax.psum_scatter(subtotal, axis, scatter_dimension=0, tiled=True)
    return subtotal


def local(kernel, basis, responses):
    highest = lax.Precision.HIGHEST
    row_count = kernel.shape[0] * lax.axis_size(ROW)
    resp_count = responses.shape[1] * lax.axis_size("col")
    root_rows = math.sqrt(row_count)
    partial_proj = jnp.dot(
        kernel, lax.all_gather(basis, ROW, axis=1, tiled=True), precision=highest
    )
    projected = taken_together(partial_proj, "col")
    gram_part = jnp.dot(projected.T, projected, precision=highest) / row_count
    gram_mat = taken_together(gram_part, ROW)
    factor = jnp.linalg.cholesky(gram_mat)
    scores = jax.scipy.linalg.solve_triangular(factor, projected.T, lower=True).T
    weight_part = jnp.dot(responses.T, scores, precision=highest) / root_rows
    weights = taken_together(weight_part, ROW)
    next_part = jnp.dot(responses, weights, precision=highest) / math.sqrt(resp_count)
    basis_next = taken_together(next_part, "col")
    loadings = summed_rows(jnp.dot(scores.T, kernel, precision=highest) / root_rows, ROW)
    all_loadings = lax.all_gather(loadings, ROW, axis=0, tiled=True)
    deflated = kernel - jnp.dot(scores, all_loadings, precision=highest) / root_rows
    return (scores, loadings, weights, deflated, basis_next)


def solution(mesh):
    finer = Mesh(mesh.devices.reshape(4, 8, mesh.shape["col"]), ("row_0", "row_1", "col"))
    in_specs = (P(ROW, "col"), P("col", ROW), P(ROW, "col"))
    out_specs = (P(ROW, None), P(ROW, "col"), P("col", None), P(ROW, "col"), P(ROW, None))
    return jax.shard_map(local, mesh=finer, in_specs=in_specs, out_specs=out_specs, check_vma=False)
```

profile of v0, /device:TPU:8, one launch (start us, length us, event | category | flops | bytes accessed | tf_op | source)
XLA Modules:
  0.0 430.5 jit_solution(12463068032764752603)
XLA Ops:
  7.2 0.7 all-gather.5.cloned.1.call-update
  8.0 87.2 %all-gather.5.cloned.1.call-done = f32[32,4,8192]{2,1,0:T(4,128)} async-done(((f32[1,4,8192]{2,1,0:T(4,128)}), f32[32,4,8192]{2,1,0:T(4,128)}) %all-gather.5.cloned.1.call-update) | async-done | bytes 4194320 | tf_op jit(solution)/shard_map/all_gather | solution.py:33
  95.2 5.3 %reshape.25 = f32[128,8192]{1,0:T(8,128)} reshape(f32[32,4,8192]{2,1,0:T(4,128)} %all-gather.5.cloned.1.call-done) | data formatting | bytes 8388608
  100.5 6.2 %fusion.7 = f32[64,128]{1,0:T(8,128)S(1)} fusion(f32[64,8192]{1,0:T(8,128)S(1)} %copy-done.1, f32[128,8192]{1,0:T(8,128)} %reshape.25), kind=kOutput, calls=%fused_computation.19 | convolution fusion | flops 805306368 | bytes 6324224 | tf_op jit(solution)/shard_map/dot_general | solution.py:32
  106.7 10.7 %all_to_all.20 = f32[8,64,128]{2,1,0:T(8,128)S(1)} all-to-all(f32[8,64,128]{2,1,0:T(8,128)S(1)} %broadcast_in_dim.10), channel_id=1, replica_groups=mesh['row_0'=4,'row_1'=8,'col'=8] {'col'}, dimensions={0} | all-to-all | bytes 524288 | tf_op jit(solution)/shard_map/all_to_all | solution.py:13
  117.4 0.3 convolution_multiply_fusion.2
  117.7 0.2 broadcast_in_dim.11
  117.9 56.2 %all_to_all.21 = f32[32,128,128]{2,1,0:T(8,128)} all-to-all(f32[32,128,128]{2,1,0:T(8,128)S(1)} %broadcast_in_dim.11), channel_id=1, replica_groups=mesh['row_0'=4,'row_1'=8,'col'=8] {'row_0','row_1'}, dimensions={0} | all-to-all | bytes 4194304 | tf_op jit(solution)/shard_map/all_to_all | solution.py:13
  174.1 1.7 reduce_sum.37
  175.8 0.1 copy.10
  175.9 11.7 %cholesky.16 = f32[128,128]{1,0:T(8,128)S(1)} custom-call(f32[128,128]{1,0:T(8,128)S(1)} %fusion.6), custom_call_target="Cholesky" | custom-call | tf_op jit(solution)/shard_map/jit(cholesky)/cholesky | solution.py:38
  187.7 0.6 compare_reduce_fusion
  188.3 0.7 fusion.3
  189.0 9.8 %custom-call.7 = f32[1,128,128]{1,2,0:T(8,128)S(1)} custom-call(f32[1,128,128]{2,1,0:T(8,128)S(1)} %fusion.3), custom_call_target="InvertDiagBlocksLowerTriangular" | custom-call | tf_op jit(solution)/shard_map/jit(_solve_triangular)/triangular_solve | solution.py:39
  198.8 0.2 fusion.4
  199.0 5.1 %convolution_multiply_fusion = f32[128,8192]{1,0:T(8,128)} fusion(f32[128,64]{0,1:T(8,128)S(1)} %fusion.4, f32[64,8192]{1,0:T(8,128)S(1)} %copy-done.1), kind=kOutput, calls=%fused_computation | convolution fusion | flops 806354944 | bytes 6324224 | tf_op jit(solution)/shard_map/dot_general | solution.py:44
  204.1 0.0 all-reduce.3.cloned.1.call-start
  204.1 45.0 %reduce-scatter.2.cloned.1.call-done = f32[32,8192]{1,0:T(8,128)} async-done(((f32[128,8192]{1,0:T(8,128)}), f32[32,8192]{1,0:T(8,128)}) %reduce-scatter.2.cloned.1.call-update) | async-done | bytes 1048592 | tf_op jit(solution)/shard_map/reduce_scatter | solution.py:23
  249.2 0.6 dynamic-slice
  250.4 76.9 %all-reduce.3.cloned.1.call-done = f32[32,8192]{1,0:T(8,128)} async-done(((f32[32,8192]{1,0:T(8,128)}), f32[32,8192]{1,0:T(8,128)}) %all-reduce.3.cloned.1.call-update) | async-done | bytes 1048592
  327.3 1.6 fusion.21
  328.9 0.2 fusion.2
  329.2 0.1 broadcast_in_dim.12
  329.3 33.8 %all_to_all.22 = f32[32,64,128]{2,1,0:T(8,128)S(1)} all-to-all(f32[32,64,128]{2,1,0:T(8,128)S(1)} %broadcast_in_dim.12), channel_id=1, replica_groups=mesh['row_0'=4,'row_1'=8,'col'=8] {'row_0','row_1'}, dimensions={0} | all-to-all | bytes 2097152 | tf_op jit(solution)/shard_map/all_to_all | solution.py:13
  363.1 0.1 reduce_sum.38
  363.2 0.2 fusion.1
  363.4 10.7 %all_to_all.23 = f32[8,64,128]{2,1,0:T(8,128)S(1)} all-to-all(f32[8,64,128]{2,1,0:T(8,128)S(1)} %broadcast_in_dim.13), channel_id=1, replica_groups=mesh['row_0'=4,'row_1'=8,'col'=8] {'col'}, dimensions={0} | all-to-all | bytes 524288 | tf_op jit(solution)/shard_map/all_to_all | solution.py:13
  374.1 0.6 reduce_sum.39
  374.7 1.6 constant_dynamic-slice_fusion
  376.4 36.4 %all-gather.7.cloned.1.call-done = f32[32,4,8192]{2,1,0:T(4,128)} async-done(((f32[1,4,8192]{2,1,0:T(4,128)}), f32[32,4,8192]{2,1,0:T(4,128)}) %all-gather.7.cloned.1.call-update) | async-done | bytes 4194320 | tf_op jit(solution)/shard_map/all_gather | solution.py:45
  412.8 5.3 %reshape.27 = f32[128,8192]{1,0:T(8,128)} reshape(f32[32,4,8192]{2,1,0:T(4,128)} %all-gather.7.cloned.1.call-done) | data formatting | bytes 8388608
  418.1 5.9 %fusion = f32[64,8192]{1,0:T(8,128)} fusion(f32[64,8192]{1,0:T(8,128)S(1)} %copy-done.1, f32[128,64]{0,1:T(8,128)S(1)} %fusion.4, f32[128,8192]{1,0:T(8,128)} %reshape.27), kind=kOutput, calls=%fused_computation.2 | convolution fusion | flops 806354944 | bytes 8421376 | tf_op jit(solution)/shard_map/dot_general | solution.py:46
  (21 shorter events, 0.3 us)
Async XLA Ops:
  7.2 321.8 %copy-start = (f32[64,64]{1,0:T(8,128)S(1)}, f32[64,64]{1,0:T(8,128)}, u32[]{:S(2)}) copy-start(f32[64,64]{1,0:T(8,128)} %param.5) | copy-start | bytes 49156
  7.2 88.0 %all-gather.5.cloned.1.call-start = ((), (), s32[]{:S(2)}) async-start(), calls=%async_computation.6 | async-start | bytes 4325376 | tf_op jit(solution)/shard_map/all_gather | solution.py:33
  7.9 92.6 %copy-start.1 = (f32[64,8192]{1,0:T(8,128)S(1)}, f32[64,8192]{1,0:T(8,128)}, u32[]{:S(2)}) copy-start(f32[64,8192]{1,0:T(8,128)} %param.3) | copy-start | bytes 6291460
  7.9 241.2 %reduce-scatter.2.cloned.1.call-start = ((), (), s32[]{:S(2)}) async-start(), calls=%async_computation.5 | async-start | bytes 5242880 | tf_op jit(solution)/shard_map/reduce_scatter | solution.py:23
  199.0 219.1 %copy-start.2 = (f32[128,64]{0,1:T(8,128)}, f32[128,64]{0,1:T(8,128)S(1)}, u32[]{:S(2)}) copy-start(f32[128,64]{0,1:T(8,128)S(1)} %fusion.4) | copy-start | bytes 98308
  204.1 45.1 %copy-start.4 = (u32[256]{0:T(256)S(1)}, u32[256]{0:T(256)}, u32[]{:S(2)}) copy-start(u32[256]{0:T(256)} %constant.60) | copy-start | bytes 3076
  204.1 123.2 %all-reduce.3.cloned.1.call-start = ((), (), s32[]{:S(2)}) async-start(), calls=%async_computation.8 | async-start | bytes 2097152
  249.1 163.7 %all-gather.7.cloned.1.call-start = ((), (), s32[]{:S(2)}) async-start(), calls=%async_computation.7 | async-start | bytes 4325376 | tf_op jit(solution)/shard_map/all_gather | solution.py:45
  363.2 54.9 %copy-start.3 = (f32[64,128]{1,0:T(8,128)}, f32[64,128]{1,0:T(8,128)S(1)}, u32[]{:S(2)}) copy-start(f32[64,128]{1,0:T(8,128)S(1)} %reduce_sum.38) | copy-start | bytes 98308
Sparse Core Ops, SparseCore 0:
  10.6 84.5 all-gather.4
  204.2 44.8 reduce-scatter.1
  251.4 75.7 all-reduce.2
  330.3 82.4 all-gather.6
where the time goes:
time: 431 us; the launch traced here: 430 us
  waiting for transfers between devices  246 us (57%)
  blocking collectives  111 us (26%)
  other arithmetic  25.3 us (6%)
  matrix products  18 us (4%)
  local copies, waits for them, and re-layouts  14.9 us (3%)
  between operations  14.6 us (3%)
    all_to_all x4, blocking collectives, sent_to_all(): lax.all_to_all(jnp.broadcast_to(x[None], (devices, *x.shape)), axis, 0, 0...  111 us
    all_gather x1, waiting for transfers between devices, local(): lax.all_gather(basis, ROW, axis=1, tiled=True)  87.2 us
    unnamed x5, waiting for transfers between devices  77.6 us
    reduce_scatter x1, waiting for transfers between devices, summed_rows(): subtotal = lax.psum_scatter(subtotal, axis, scatter_dimension=0, tiled=True)  45 us
    all_gather x1, waiting for transfers between devices, local(): all_loadings = lax.all_gather(loadings, ROW, axis=0, tiled=True)  36.4 us
    unnamed x15, local copies, waits for them, and re-layouts  14.4 us
    another operation x3, other arithmetic, local(): factor = jnp.linalg.cholesky(gram_mat)  12.4 us
    another operation x2, other arithmetic, local(): jax.scipy.linalg.solve_triangular(factor, projected.T, lower=True)  10.5 us
  transfers between devices with their start and end apart: 4, of which 4 were waited for; matrix products, arithmetic and copies ran while one was open for 1% of the time, Pallas kernels for 0%

commit v1 on v0

--- a/solution.py
+++ b/solution.py
@@ -42,7 +42,9 @@
     next_part = jnp.dot(responses, weights, precision=highest) / math.sqrt(resp_count)
     basis_next = taken_together(next_part, "col")
     loadings = summed_rows(jnp.dot(scores.T, kernel, precision=highest) / root_rows, ROW)
-    all_loadings = lax.all_gather(loadings, ROW, axis=0, tiled=True)
+    all_loadings = jnp.concatenate(
+        lax.all_to_all(jnp.stack([loadings] * lax.axis_size(ROW)), ROW, 0, 0), axis=0
+    )
     deflated = kernel - jnp.dot(scores, all_loadings, precision=highest) / root_rows
     return (scores, loadings, weights, deflated, basis_next)
 

time: 431 us -> 458 us (1.063)
  waiting for transfers between devices: 246 us -> 299 us
  blocking collectives: 111 us -> 66.8 us
  starting transfers between devices: 0.16 us -> 16.7 us
    all_to_all x0 -> x3, waiting for transfers between devices: none -> 91.5 us  [the longest x1 91.5 us: local(): lax.all_to_all(jnp.stack([loadings] * lax.axis_size(ROW)), ROW, 0, 0)]
    all_to_all x4 -> x2, blocking collectives: 111 us -> 66.8 us  [sent_to_all(): lax.all_to_all(jnp.broadcast_to(x[None], (devices, *x.shape)), axis, 0, 0...]
    all_gather x1 -> x0, waiting for transfers between devices: 36.4 us -> none  [local(): all_loadings = lax.all_gather(loadings, ROW, axis=0, tiled=True)]
    all_to_all x0 -> x3, starting transfers between devices: none -> 16.6 us  [the longest x2 9.49 us: sent_to_all(): lax.all_to_all(jnp.broadcast_to(x[None], (devices, *x.shape)), axis, 0, 0...]
    unnamed x15, local copies, waits for them, and re-layouts: 14.4 us -> 6.88 us
    unnamed x5 -> x4, waiting for transfers between devices: 77.6 us -> 71 us
    reshape x0 -> x1, local copies, waits for them, and re-layouts: none -> 5.28 us  [local(): jnp.concatenate(lax.all_to_all(jnp.stack([loadings] * lax.axis_size(ROW))...]
  transfers between devices with their start and end apart: 4 -> 6, of which waited for: 4 -> 4; matrix products, arithmetic and copies ran while one was open for 1% -> 1% of each run, Pallas kernels for 0% -> 0%
where the time goes in v1:
time: 458 us
  waiting for transfers between devices  299 us (65%)
  blocking collectives  66.8 us (15%)
  other arithmetic  25.3 us (6%)
  matrix products  18 us (4%)
  local copies, waits for them, and re-layouts  17.2 us (4%)
  starting transfers between devices  16.7 us (4%)
  between operations  14.6 us (3%)
    all_to_all x1, waiting for transfers between devices, local(): lax.all_to_all(jnp.stack([loadings] * lax.axis_size(ROW)), ROW, 0, 0)  91.5 us
    all_gather x1, waiting for transfers between devices, local(): lax.all_gather(basis, ROW, axis=1, tiled=True)  87.2 us
    unnamed x4, waiting for transfers between devices  71 us
    all_to_all x2, blocking collectives, sent_to_all(): lax.all_to_all(jnp.broadcast_to(x[None], (devices, *x.shape)), axis, 0, 0...  66.8 us
    reduce_scatter x1, waiting for transfers between devices, summed_rows(): subtotal = lax.psum_scatter(subtotal, axis, scatter_dimension=0, tiled=True)  49.4 us
    another operation x3, other arithmetic, local(): factor = jnp.linalg.cholesky(gram_mat)  12.4 us
    another operation x2, other arithmetic, local(): jax.scipy.linalg.solve_triangular(factor, projected.T, lower=True)  10.5 us
    all_to_all x2, starting transfers between devices, sent_to_all(): lax.all_to_all(jnp.broadcast_to(x[None], (devices, *x.shape)), axis, 0, 0...  9.49 us
  transfers between devices with their start and end apart: 6, of which 4 were waited for; matrix products, arithmetic and copies ran while one was open for 1% of the time, Pallas kernels for 0%

profile of v1, /device:TPU:8, one launch (start us, length us, event | category | flops | bytes accessed | tf_op | source)
XLA Modules:
  0.0 457.8 jit_solution(15297981898058067649)
XLA Ops:
  7.2 0.7 all-gather.3.cloned.1.call-update
  8.0 87.2 %all-gather.3.cloned.1.call-done = f32[32,4,8192]{2,1,0:T(4,128)} async-done(((f32[1,4,8192]{2,1,0:T(4,128)}), f32[32,4,8192]{2,1,0:T(4,128)}) %all-gather.3.cloned.1.call-update) | async-done | bytes 4194320 | tf_op jit(solution)/shard_map/all_gather | solution.py:33
  95.2 5.3 %reshape.31 = f32[128,8192]{1,0:T(8,128)} reshape(f32[32,4,8192]{2,1,0:T(4,128)} %all-gather.3.cloned.1.call-done) | data formatting | bytes 8388608
  100.5 6.2 %fusion.7 = f32[64,128]{1,0:T(8,128)S(1)} fusion(f32[64,8192]{1,0:T(8,128)S(1)} %copy-done.1, f32[128,8192]{1,0:T(8,128)} %reshape.31), kind=kOutput, calls=%fused_computation.19 | convolution fusion | flops 805306368 | bytes 6324224 | tf_op jit(solution)/shard_map/dot_general | solution.py:32
  106.7 10.7 %all_to_all.25 = f32[8,64,128]{2,1,0:T(8,128)S(1)} all-to-all(f32[8,64,128]{2,1,0:T(8,128)S(1)} %broadcast_in_dim.10), channel_id=1, replica_groups=mesh['row_0'=4,'row_1'=8,'col'=8] {'col'}, dimensions={0} | all-to-all | bytes 524288 | tf_op jit(solution)/shard_map/all_to_all | solution.py:13
  117.4 0.3 convolution_multiply_fusion.2
  117.7 0.2 broadcast_in_dim.11
  117.9 56.2 %all_to_all.26 = f32[32,128,128]{2,1,0:T(8,128)} all-to-all(f32[32,128,128]{2,1,0:T(8,128)S(1)} %broadcast_in_dim.11), channel_id=1, replica_groups=mesh['row_0'=4,'row_1'=8,'col'=8] {'row_0','row_1'}, dimensions={0} | all-to-all | bytes 4194304 | tf_op jit(solution)/shard_map/all_to_all | solution.py:13
  174.1 1.7 reduce_sum.37
  175.8 0.1 copy.10
  175.9 11.7 %cholesky.16 = f32[128,128]{1,0:T(8,128)S(1)} custom-call(f32[128,128]{1,0:T(8,128)S(1)} %fusion.6), custom_call_target="Cholesky" | custom-call | tf_op jit(solution)/shard_map/jit(cholesky)/cholesky | solution.py:38
  187.7 0.6 compare_reduce_fusion
  188.3 0.7 fusion.3
  189.0 9.8 %custom-call.7 = f32[1,128,128]{1,2,0:T(8,128)S(1)} custom-call(f32[1,128,128]{2,1,0:T(8,128)S(1)} %fusion.3), custom_call_target="InvertDiagBlocksLowerTriangular" | custom-call | tf_op jit(solution)/shard_map/jit(_solve_triangular)/triangular_solve | solution.py:39
  198.8 0.2 fusion.4
  199.0 5.1 %convolution_multiply_fusion = f32[128,8192]{1,0:T(8,128)} fusion(f32[128,64]{0,1:T(8,128)S(1)} %fusion.4, f32[64,8192]{1,0:T(8,128)S(1)} %copy-done.1), kind=kOutput, calls=%fused_computation | convolution fusion | flops 806354944 | bytes 6324224 | tf_op jit(solution)/shard_map/dot_general | solution.py:44
  204.1 0.2 fusion.2
  204.3 1.1 broadcast_in_dim.12
  205.4 4.9 %all-to-all-start.2 = ((f32[32,64,128]{2,1,0:T(8,128)}), f32[32,64,128]{2,1,0:T(8,128)S(1)}, u32[]{:S(2)}, u32[]{:S(2)}) async-start(f32[32,64,128]{2,1,0:T(8,128)} %broadcast_in_dim.12), calls=%async_computation.3 | async-start | bytes 2097152 | tf_op jit(solution)/shard_map/all_to_all | solution.py:13
  210.4 49.4 %reduce-scatter.2.cloned.1.call-done = f32[32,8192]{1,0:T(8,128)} async-done(((f32[128,8192]{1,0:T(8,128)}), f32[32,8192]{1,0:T(8,128)}) %reduce-scatter.2.cloned.1.call-update) | async-done | bytes 1048592 | tf_op jit(solution)/shard_map/reduce_scatter | solution.py:23
  259.9 0.6 dynamic-slice
  261.2 0.2 fusion.1
  261.4 0.7 broadcast_in_dim.13
  262.1 4.6 all-to-all-start.4
  266.7 70.3 %all-reduce.3.cloned.1.call-done = f32[32,8192]{1,0:T(8,128)} async-done(((f32[32,8192]{1,0:T(8,128)}), f32[32,8192]{1,0:T(8,128)}) %all-reduce.3.cloned.1.call-update) | async-done | bytes 1048592
  336.9 1.0 constant_dynamic-slice_fusion
  337.9 2.9 stack.2
  340.9 7.1 %all-to-all-start.3 = ((f32[32,4,8192]{2,1,0:T(4,128)}), f32[32,4,8192]{2,1,0:T(4,128)}, u32[]{:S(2)}, u32[]{:S(2)}) async-start(f32[32,4,8192]{2,1,0:T(4,128)} %stack.2), calls=%async_computation.4 | async-start | bytes 8388608 | tf_op jit(solution)/shard_map/all_to_all | solution.py:46
  348.0 0.6 reduce_sum.39
  348.6 91.5 %all-to-all-done.3 = f32[32,4,8192]{2,1,0:T(4,128)} async-done(((f32[32,4,8192]{2,1,0:T(4,128)}), f32[32,4,8192]{2,1,0:T(4,128)}, u32[]{:S(2)}, u32[]{:S(2)}) %all-to-all-start.3) | async-done | bytes 4194336 | tf_op jit(solution)/shard_map/all_to_all | solution.py:46
  440.1 5.3 %reshape.29 = f32[128,8192]{1,0:T(8,128)} reshape(f32[32,4,8192]{2,1,0:T(4,128)} %all-to-all-done.3) | data formatting | bytes 8388608 | tf_op jit(solution)/shard_map/reshape | solution.py:45
  445.4 5.9 %fusion = f32[64,8192]{1,0:T(8,128)} fusion(f32[64,8192]{1,0:T(8,128)S(1)} %copy-done.1, f32[128,64]{0,1:T(8,128)S(1)} %fusion.4, f32[128,8192]{1,0:T(8,128)} %reshape.29), kind=kOutput, calls=%fused_computation.2 | convolution fusion | flops 806354944 | bytes 8421376 | tf_op jit(solution)/shard_map/dot_general | solution.py:48
  (24 shorter events, 0.3 us)
Async XLA Ops:
  7.2 196.9 %copy-start = (f32[64,64]{1,0:T(8,128)S(1)}, f32[64,64]{1,0:T(8,128)}, u32[]{:S(2)}) copy-start(f32[64,64]{1,0:T(8,128)} %param.5) | copy-start | bytes 49156
  7.2 88.0 %all-gather.3.cloned.1.call-start = ((), (), s32[]{:S(2)}) async-start(), calls=%async_computation.7 | async-start | bytes 4325376 | tf_op jit(solution)/shard_map/all_gather | solution.py:33
  7.9 92.6 %copy-start.1 = (f32[64,8192]{1,0:T(8,128)S(1)}, f32[64,8192]{1,0:T(8,128)}, u32[]{:S(2)}) copy-start(f32[64,8192]{1,0:T(8,128)} %param.3) | copy-start | bytes 6291460
  7.9 251.9 %reduce-scatter.2.cloned.1.call-start = ((), (), s32[]{:S(2)}) async-start(), calls=%async_computation.6 | async-start | bytes 5242880 | tf_op jit(solution)/shard_map/reduce_scatter | solution.py:23
  199.0 246.4 %copy-start.2 = (f32[128,64]{0,1:T(8,128)}, f32[128,64]{0,1:T(8,128)S(1)}, u32[]{:S(2)}) copy-start(f32[128,64]{0,1:T(8,128)S(1)} %fusion.4) | copy-start | bytes 98308
  204.1 55.8 %copy-start.5 = (u32[256]{0:T(256)S(1)}, u32[256]{0:T(256)}, u32[]{:S(2)}) copy-start(u32[256]{0:T(256)} %constant.60) | copy-start | bytes 3076
  205.4 55.7 %all-to-all-start.2 = ((f32[32,64,128]{2,1,0:T(8,128)}), f32[32,64,128]{2,1,0:T(8,128)S(1)}, u32[]{:S(2)}, u32[]{:S(2)}) async-start(f32[32,64,128]{2,1,0:T(8,128)} %broadcast_in_dim.12), calls=%async_computation.3 | async-start | bytes 2097152 | tf_op jit(solution)/shard_map/all_to_all | solution.py:13
  210.4 126.6 %all-reduce.3.cloned.1.call-start = ((), (), s32[]{:S(2)}) async-start(), calls=%async_computation.8 | async-start | bytes 2097152
  261.2 79.6 %copy-start.4 = (f32[64,128]{1,0:T(8,128)}, f32[64,128]{1,0:T(8,128)S(1)}, u32[]{:S(2)}) copy-start(f32[64,128]{1,0:T(8,128)S(1)} %reduce_sum.38) | copy-start | bytes 98308
  262.1 75.8 %all-to-all-start.4 = ((f32[8,64,128]{2,1,0:T(8,128)}), f32[8,64,128]{2,1,0:T(8,128)S(1)}, u32[]{:S(2)}, u32[]{:S(2)}) async-start(f32[8,64,128]{2,1,0:T(8,128)} %broadcast_in_dim.13), calls=%async_computation.5 | async-start | bytes 524288 | tf_op jit(solution)/shard_map/all_to_all | solution.py:13
  337.9 2.9 copy-start.3
  340.9 99.2 %all-to-all-start.3 = ((f32[32,4,8192]{2,1,0:T(4,128)}), f32[32,4,8192]{2,1,0:T(4,128)}, u32[]{:S(2)}, u32[]{:S(2)}) async-start(f32[32,4,8192]{2,1,0:T(4,128)} %stack.2), calls=%async_computation.4 | async-start | bytes 8388608 | tf_op jit(solution)/shard_map/all_to_all | solution.py:46
Sparse Core Ops, SparseCore 0:
  10.6 84.5 all-gather.2
  204.2 55.5 reduce-scatter.1
  262.2 74.6 all-reduce.2
